TPU v7x, 512 devices: a whole 4x8x8 slice. The times are simulated.
512 devices in a mesh: vox: 32 (over z_lo, y), opt: 16 (over z_hi, x, core).
Axes of the slice: x: 4, y: 8, z: 8 (z_hi: 2, z_lo: 4; z = z_hi * 4 + z_lo), core: 2. Of those that a mesh axis runs over, the one named last changes fastest.
Arguments:
- source_fields: bfloat16 [1024, 24576], P('opt', 'vox'), may hold values from -6 to 6
- detector_fields: bfloat16 [4096, 24576], P('opt', 'vox'), may hold values from -6 to 6
- measured: float32 [1024, 4096], P('vox', 'opt'), may hold values from -6 to 6
- valid_pair: int32 [1024, 4096], P('vox', 'opt'), may hold values 0 or 1
- weight_class: int32 [1024, 4096], P('vox', 'opt'), may hold values from 0 to 3
- absorption: float32 [24576], P('vox'), may hold values from 0 to 1
Outputs:
- absorption_out: float32 [24576], P('vox')
- residual_out: float32 [1024, 4096], P('vox', 'opt')
All inputs are finite; a program needn't handle non-finite values. No bound on the sum of `valid_pair` on one device may be relied on, other than what follows from the above.
Results may differ from a plain program's by a relative error of at most 0.0026.
Values may be sent and summed in bfloat16 or wider, within the bound.
No kernel may reach another device: no remote copies, remote signals or barrier semaphores. Data moves between devices by JAX's collectives and lax.ppermute only.
A program may use at most 64 MiB of HBM per device.

v0:
```python
import jax
import jax.numpy as jnp
from jax import lax
from jax.sharding import Mesh
from jax.sharding import PartitionSpec as P


NS = 1024
ND = 4096
ITERS = 2
AXES = ("z_mid", "z_low", "y", "z_hi", "x", "core")
VOX = ("z_mid", "z_low", "y")
OPT = ("z_hi", "x", "core")
SUM = ("z_low", "y")
REST = ("z_mid", "z_hi", "x")
BF16 = jnp.bfloat16
SWAP = [(0, 1), (1, 0)]


def everywhere(block, axes, count):
    return lax.all_to_all(jnp.broadcast_to(block[None], (count,) + block.shape), axes, 0, 0)


def ordered(first, own, other):
    return jnp.where(first, own, other), jnp.where(first, other, own)


def gather_sources(block, aligned):
    rows, cols = block.shape
    first = lax.ppermute(block, ("z_mid", "z_hi"), [(0, 0), (1, 2), (2, 1), (3, 3)])
    second = lax.ppermute(block, ("z_mid", "z_hi"), [(0, 1), (1, 3), (2, 0), (3, 2)])
    pieces = jnp.stack(ordered(aligned, first, second))
    along = everywhere(pieces, "x", 4)
    return [
        lax.all_gather(along[:, k], "core", axis=1).reshape(8 * rows, cols) for k in range(2)
    ]


def local(source_fields, detector_fields, measured, valid_pair, weight_class, absorption):
    cols = absorption.shape[0]
    voxels = cols * 32
    own_rows, own_cols = measured.shape
    pred_scale = 1.0 / jnp.sqrt(jnp.float32(voxels))
    grad_scale = jnp.sqrt(jnp.float32(voxels)) / (jnp.float32(NS) * jnp.float32(ND))
    low = lax.axis_index("z_mid") == 0
    maskf = valid_pair.astype(jnp.float32) / (1.0 + weight_class.astype(jnp.float32))

    sources = gather_sources(source_fields, lax.axis_index("z_mid") == lax.axis_index("z_hi"))
    detectors = [detector_fields, lax.ppermute(detector_fields, "z_mid", SWAP)]
    mu_now = [absorption, lax.ppermute(absorption, "z_mid", SWAP)]

    weighted = None
    for _ in range(ITERS):
        partial_pred = 0.0
        for s, d, mu in zip(sources, detectors, mu_now):
            scaled = (d * mu[None, :]).astype(BF16)
            partial_pred = partial_pred + lax.dot_general(
                s, scaled, (((1,), (1,)), ((), ())), preferred_element_type=jnp.float32
            )
        sent = partial_pred.astype(BF16).reshape(16, own_rows, own_cols)
        got = lax.all_to_all(sent, SUM, 0, 0)
        predicted = jnp.sum(got.astype(jnp.float32), axis=0)
        weighted = maskf * (predicted * pred_scale - measured)
        weighted_b = weighted.astype(BF16)
        all_weighted = everywhere(weighted_b, SUM, 16).reshape(16 * own_rows, own_cols)
        terms = [
            jnp.sum(jnp.dot(all_weighted, d, preferred_element_type=jnp.float32) * s, axis=0)
            for s, d in zip(sources, detectors)
        ]
        terms = jnp.stack(ordered(low, *terms)).reshape(2 * cols // 128, 128)
        total = jnp.sum(lax.all_gather(terms, "core", axis=0), axis=0)
        total = jnp.sum(everywhere(total, REST, 16), axis=0).reshape(2, cols)
        gradient = [g * grad_scale for g in ordered(low, total[0], total[1])]
        mu_now = [jnp.maximum(mu - 2.0 * g, 0.0) for mu, g in zip(mu_now, gradient)]
    return (mu_now[0], weighted)


def solution(mesh):
    fine = Mesh(mesh.devices.reshape(2, 2, 8, 2, 4, 2), AXES)
    placed = (P(OPT, VOX), P(OPT, VOX), P(VOX, OPT), P(VOX, OPT), P(VOX, OPT), P(VOX))
    return jax.shard_map(
        local, mesh=fine, in_specs=placed, out_specs=(P(VOX), P(VOX, OPT)), check_vma=False
    )
```

profile of v0, /device:TPU:1, one launch (start us, length us, event | category | flops | bytes accessed | tf_op | source)
XLA Modules:
  0.0 147.9 jit_solution(3495052924804540737)
XLA Ops:
  0.6 1.6 %collective-permute-start = (bf16[64,768]{1,0:T(8,128)(2,1)}, bf16[64,768]{1,0:T(8,128)(2,1)S(1)}, u32[]{:S(2)}, u32[]{:S(2)}) collective-permute-start(bf16[64,768]{1,0:T(8,128)(2,1)} %param.6), channel_id=1, source_target_pairs={{0,0},{8,256},{256,8},{264,264},{1,1},{9,257},{257,9},{265,265},{2... | collective-permute-start | bytes 294920 | tf_op jit(solution)/shard_map/ppermute | solution.py:30
  2.2 11.8 %collective-permute-start.1 = (bf16[64,768]{1,0:T(8,128)(2,1)}, bf16[64,768]{1,0:T(8,128)(2,1)S(1)}, u32[]{:S(2)}, u32[]{:S(2)}) collective-permute-start(bf16[64,768]{1,0:T(8,128)(2,1)} %param.6), channel_id=1, source_target_pairs={{0,8},{8,264},{256,0},{264,256},{1,9},{9,265},{257,1},{265,257},{2... | collective-permute-start | bytes 294920 | tf_op jit(solution)/shard_map/ppermute | solution.py:31
  14.0 2.9 %collective-permute-done.1 = bf16[64,768]{1,0:T(8,128)(2,1)S(1)} collective-permute-done((bf16[64,768]{1,0:T(8,128)(2,1)}, bf16[64,768]{1,0:T(8,128)(2,1)S(1)}, u32[]{:S(2)}, u32[]{:S(2)}) %collective-permute-start.1) | collective-permute-done | bytes 98336 | tf_op jit(solution)/shard_map/ppermute | solution.py:31
  17.0 0.9 broadcast_in_dim.10
  17.9 4.1 %all-to-all-start = ((bf16[4,2,64,768]{3,2,1,0:T(8,128)(2,1)}), bf16[4,2,64,768]{3,2,1,0:T(8,128)(2,1)S(1)}, u32[]{:S(2)}, u32[]{:S(2)}) async-start(bf16[4,2,64,768]{3,2,1,0:T(8,128)(2,1)} %broadcast_in_dim.10), calls=%async_computation | async-start | bytes 1572864 | tf_op jit(solution)/shard_map/all_to_all | solution.py:21
  22.1 10.0 %collective-permute-start.2 = (bf16[256,768]{1,0:T(8,128)(2,1)S(1)}, bf16[256,768]{1,0:T(8,128)(2,1)S(1)}, u32[]{:S(2)}, u32[]{:S(2)}) collective-permute-start(bf16[256,768]{1,0:T(8,128)(2,1)S(1)} %copy-done), channel_id=1, source_target_pairs={{0,256},{256,0},{1,257},{257,1},{2,258},{258,2},{3,259},{259,3},{4... | collective-permute-start | bytes 1179656 | tf_op jit(solution)/shard_map/ppermute | solution.py:49
  32.0 1.9 %collective-permute-start.3 = (f32[768]{0:T(1024)S(1)}, f32[768]{0:T(1024)S(1)}, u32[]{:S(2)}, u32[]{:S(2)}) collective-permute-start(f32[768]{0:T(1024)S(1)} %copy-done.4), channel_id=1, source_target_pairs={{0,256},{256,0},{1,257},{257,1},{2,258},{258,2},{3,259},{259,3},{4... | collective-permute-start | bytes 9224 | tf_op jit(solution)/shard_map/ppermute | solution.py:50
  34.0 0.1 fusion.27
  34.0 3.3 %all_gather.12 = bf16[4,2,64,768]{3,2,1,0:T(8,128)(2,1)S(1)} all-gather(bf16[4,1,64,768]{3,2,1,0:T(8,128)(2,1)S(1)} %get-tuple-element.4), channel_id=1, replica_groups=mesh['z_mid'=2,'z_low'=2,'y'=8,'z_hi'=2,'x'=4,'core'=2] {'core'}, dimensions={1}, use_global_device_ids=true | all-gather | bytes 1179648 | tf_op jit(solution)/shard_map/all_gather | solution.py:35
  37.4 0.4 fusion.14
  37.8 2.4 %all_gather.13 = bf16[4,2,64,768]{3,2,1,0:T(8,128)(2,1)S(1)} all-gather(bf16[4,1,64,768]{3,2,1,0:T(8,128)(2,1)S(1)} %get-tuple-element.5), channel_id=1, replica_groups=mesh['z_mid'=2,'z_low'=2,'y'=8,'z_hi'=2,'x'=4,'core'=2] {'core'}, dimensions={1}, use_global_device_ids=true | all-gather | bytes 1179648 | tf_op jit(solution)/shard_map/all_gather | solution.py:35
  40.1 10.0 %collective-permute-done.3 = f32[768]{0:T(1024)S(1)} collective-permute-done((f32[768]{0:T(1024)S(1)}, f32[768]{0:T(1024)S(1)}, u32[]{:S(2)}, u32[]{:S(2)}) %collective-permute-start.3) | collective-permute-done | bytes 3104 | tf_op jit(solution)/shard_map/ppermute | solution.py:50
  50.1 0.4 fusion.4
  50.5 0.0 copy-start.2
  50.6 15.6 %all_to_all.35 = bf16[16,32,256]{2,1,0:T(8,128)(2,1)S(1)} all-to-all(bf16[16,32,256]{2,1,0:T(8,128)(2,1)S(1)} %bitcast.45), channel_id=1, replica_groups=mesh['z_mid'=2,'z_low'=2,'y'=8,'z_hi'=2,'x'=4,'core'=2] {'z_low','y'}, dimensions={0} | all-to-all | bytes 524288 | tf_op jit(solution)/shard_map/all_to_all | solution.py:61
  66.3 0.7 broadcast_in_dim.11
  67.0 5.5 %all-to-all-start.2 = ((bf16[16,32,256]{2,1,0:T(8,128)(2,1)}), bf16[16,32,256]{2,1,0:T(8,128)(2,1)S(1)}, u32[]{:S(2)}, u32[]{:S(2)}) async-start(bf16[16,32,256]{2,1,0:T(8,128)(2,1)} %broadcast_in_dim.11), calls=%async_computation.2 | async-start | bytes 524288 | tf_op jit(solution)/shard_map/all_to_all | solution.py:21
  72.5 7.9 %all-to-all-done.2 = bf16[16,32,256]{2,1,0:T(8,128)(2,1)S(1)} async-done(((bf16[16,32,256]{2,1,0:T(8,128)(2,1)}), bf16[16,32,256]{2,1,0:T(8,128)(2,1)S(1)}, u32[]{:S(2)}, u32[]{:S(2)}) %all-to-all-start.2) | async-done | bytes 262176 | tf_op jit(solution)/shard_map/all_to_all | solution.py:21
  80.4 0.4 fusion
  80.8 0.4 fusion.2
  81.3 4.7 %all_gather.14 = f32[2,12,128]{2,1,0:T(8,128)S(1)} all-gather(f32[1,12,128]{2,1,0:T(8,128)S(1)} %all_gather_reshape.6), channel_id=1, replica_groups=mesh['z_mid'=2,'z_low'=2,'y'=8,'z_hi'=2,'x'=4,'core'=2] {'core'}, dimensions={0}, use_global_device_ids=true | all-gather | bytes 18432 | tf_op jit(solution)/shard_map/all_gather | solution.py:71
  86.0 15.2 %all_to_all.36 = f32[16,12,128]{2,1,0:T(8,128)S(1)} all-to-all(f32[16,12,128]{2,1,0:T(8,128)S(1)} %broadcast_in_dim.12), channel_id=1, replica_groups=mesh['z_mid'=2,'z_low'=2,'y'=8,'z_hi'=2,'x'=4,'core'=2] {'z_mid','z_hi',..., dimensions={0} | all-to-all | bytes 196608 | tf_op jit(solution)/shard_map/all_to_all | solution.py:21
  101.3 0.4 fusion.12
  101.7 0.4 fusion.5
  102.1 11.5 %all_to_all.37 = bf16[16,32,256]{2,1,0:T(8,128)(2,1)S(1)} all-to-all(bf16[16,32,256]{2,1,0:T(8,128)(2,1)S(1)} %bitcast.44), channel_id=1, replica_groups=mesh['z_mid'=2,'z_low'=2,'y'=8,'z_hi'=2,'x'=4,'core'=2] {'z_low','y'}, dimensions={0} | all-to-all | bytes 524288 | tf_op jit(solution)/shard_map/all_to_all | solution.py:61
  113.6 0.6 fusion.26
  114.3 13.0 %all_to_all.38 = bf16[16,32,256]{2,1,0:T(8,128)(2,1)S(1)} all-to-all(bf16[16,32,256]{2,1,0:T(8,128)(2,1)S(1)} %broadcast_in_dim.13), channel_id=1, replica_groups=mesh['z_mid'=2,'z_low'=2,'y'=8,'z_hi'=2,'x'=4,'core'=2] {'z_low','y'}, dimensions={0} | all-to-all | bytes 524288 | tf_op jit(solution)/shard_map/all_to_all | solution.py:21
  127.3 0.4 fusion.1
  127.7 0.4 fusion.3
  128.1 5.1 %all_gather.15 = f32[2,12,128]{2,1,0:T(8,128)S(1)} all-gather(f32[1,12,128]{2,1,0:T(8,128)S(1)} %all_gather_reshape.7), channel_id=1, replica_groups=mesh['z_mid'=2,'z_low'=2,'y'=8,'z_hi'=2,'x'=4,'core'=2] {'core'}, dimensions={0}, use_global_device_ids=true | all-gather | bytes 18432 | tf_op jit(solution)/shard_map/all_gather | solution.py:71
  133.3 14.0 %all_to_all.39 = f32[16,12,128]{2,1,0:T(8,128)S(1)} all-to-all(f32[16,12,128]{2,1,0:T(8,128)S(1)} %broadcast_in_dim.14), channel_id=1, replica_groups=mesh['z_mid'=2,'z_low'=2,'y'=8,'z_hi'=2,'x'=4,'core'=2] {'z_mid','z_hi',..., dimensions={0} | all-to-all | bytes 196608 | tf_op jit(solution)/shard_map/all_to_all | solution.py:21
  147.3 0.6 fusion.23
  (35 shorter events, 0.4 us)
Async XLA Ops:
  0.6 13.4 %collective-permute-start = (bf16[64,768]{1,0:T(8,128)(2,1)}, bf16[64,768]{1,0:T(8,128)(2,1)S(1)}, u32[]{:S(2)}, u32[]{:S(2)}) collective-permute-start(bf16[64,768]{1,0:T(8,128)(2,1)} %param.6), channel_id=1, source_target_pairs={{0,0},{8,256},{256,8},{264,264},{1,1},{9,257},{257,9},{265,265},{2... | collective-permute-start | bytes 294920 | tf_op jit(solution)/shard_map/ppermute | solution.py:30
  2.2 14.7 %collective-permute-start.1 = (bf16[64,768]{1,0:T(8,128)(2,1)}, bf16[64,768]{1,0:T(8,128)(2,1)S(1)}, u32[]{:S(2)}, u32[]{:S(2)}) collective-permute-start(bf16[64,768]{1,0:T(8,128)(2,1)} %param.6), channel_id=1, source_target_pairs={{0,8},{8,264},{256,0},{264,256},{1,9},{9,265},{257,1},{265,257},{2... | collective-permute-start | bytes 294920 | tf_op jit(solution)/shard_map/ppermute | solution.py:31
  17.9 4.2 %copy-start = (bf16[256,768]{1,0:T(8,128)(2,1)S(1)}, bf16[256,768]{1,0:T(8,128)(2,1)}, u32[]{:S(2)}) copy-start(bf16[256,768]{1,0:T(8,128)(2,1)} %param.7) | copy-start | bytes 1179652
  17.9 14.1 %copy-start.4 = (f32[768]{0:T(1024)S(1)}, f32[768]{0:T(1024)}, u32[]{:S(2)}) copy-start(f32[768]{0:T(1024)} %param.11) | copy-start | bytes 9220
  17.9 16.1 %all-to-all-start = ((bf16[4,2,64,768]{3,2,1,0:T(8,128)(2,1)}), bf16[4,2,64,768]{3,2,1,0:T(8,128)(2,1)S(1)}, u32[]{:S(2)}, u32[]{:S(2)}) async-start(bf16[4,2,64,768]{3,2,1,0:T(8,128)(2,1)} %broadcast_in_dim.10), calls=%async_computation | async-start | bytes 1572864 | tf_op jit(solution)/shard_map/all_to_all | solution.py:21
  22.1 28.0 %collective-permute-start.2 = (bf16[256,768]{1,0:T(8,128)(2,1)S(1)}, bf16[256,768]{1,0:T(8,128)(2,1)S(1)}, u32[]{:S(2)}, u32[]{:S(2)}) collective-permute-start(bf16[256,768]{1,0:T(8,128)(2,1)S(1)} %copy-done), channel_id=1, source_target_pairs={{0,256},{256,0},{1,257},{257,1},{2,258},{258,2},{3,259},{259,3},{4... | collective-permute-start | bytes 1179656 | tf_op jit(solution)/shard_map/ppermute | solution.py:49
  32.0 18.1 %collective-permute-start.3 = (f32[768]{0:T(1024)S(1)}, f32[768]{0:T(1024)S(1)}, u32[]{:S(2)}, u32[]{:S(2)}) collective-permute-start(f32[768]{0:T(1024)S(1)} %copy-done.4), channel_id=1, source_target_pairs={{0,256},{256,0},{1,257},{257,1},{2,258},{258,2},{3,259},{259,3},{4... | collective-permute-start | bytes 9224 | tf_op jit(solution)/shard_map/ppermute | solution.py:50
  50.5 15.7 %copy-start.1 = (f32[32,256]{1,0:T(8,128)S(1)}, f32[32,256]{1,0:T(8,128)}, u32[]{:S(2)}) copy-start(f32[32,256]{1,0:T(8,128)} %param.8) | copy-start | bytes 98308
  50.5 15.7 %copy-start.2 = (s32[32,256]{1,0:T(8,128)S(1)}, s32[32,256]{1,0:T(8,128)}, u32[]{:S(2)}) copy-start(s32[32,256]{1,0:T(8,128)} %param.10) | copy-start | bytes 98308
  50.5 15.7 %copy-start.3 = (s32[32,256]{1,0:T(8,128)S(1)}, s32[32,256]{1,0:T(8,128)}, u32[]{:S(2)}) copy-start(s32[32,256]{1,0:T(8,128)} %param.9) | copy-start | bytes 98308
  67.0 13.4 %all-to-all-start.2 = ((bf16[16,32,256]{2,1,0:T(8,128)(2,1)}), bf16[16,32,256]{2,1,0:T(8,128)(2,1)S(1)}, u32[]{:S(2)}, u32[]{:S(2)}) async-start(bf16[16,32,256]{2,1,0:T(8,128)(2,1)} %broadcast_in_dim.11), calls=%async_computation.2 | async-start | bytes 524288 | tf_op jit(solution)/shard_map/all_to_all | solution.py:21
where the time goes:
time: 149 us; the launch traced here: 148 us
  blocking collectives  84.9 us (57%)
  starting transfers between devices  34.9 us (23%)
  waiting for transfers between devices  20.8 us (14%)
  matrix products  3.18 us (2%)
  local copies, waits for them, and re-layouts  1.82 us (1%)
    all_to_all x3, blocking collectives, everywhere(): lax.all_to_all(jnp.broadcast_to(block[None], (count,) + block.shape), axe...  42.3 us
    all_to_all x2, blocking collectives, local(): got = lax.all_to_all(sent, SUM, 0, 0)  27.1 us
    ppermute x1, starting transfers between devices, gather_sources(): lax.ppermute(block, ('z_mid', 'z_hi'), [(0, 1), (1, 3), (2, 0), (3, 2)])  11.8 us
    ppermute x1, waiting for transfers between devices, local(): mu_now = [absorption, lax.ppermute(absorption, 'z_mid', SWAP)]  9.96 us
    ppermute x1, starting transfers between devices, local(): detectors = [detector_fields, lax.ppermute(detector_fields, 'z_mid', SWAP)]  9.96 us
    all_gather x2, blocking collectives, local(): total = jnp.sum(lax.all_gather(terms, 'core', axis=0), axis=0)  9.82 us
    all_to_all x2, starting transfers between devices, everywhere(): lax.all_to_all(jnp.broadcast_to(block[None], (count,) + block.shape), axe...  9.64 us
    all_to_all x2, waiting for transfers between devices, everywhere(): lax.all_to_all(jnp.broadcast_to(block[None], (count,) + block.shape), axe...  7.9 us
  transfers between devices with their start and end apart: 6, of which 3 were waited for; matrix products, arithmetic and copies ran while one was open for 0% of the time, Pallas kernels for 0%

commit v1 on v0

--- a/solution.py
+++ b/solution.py
@@ -50,7 +50,7 @@
     mu_now = [absorption, lax.ppermute(absorption, "z_mid", SWAP)]
 
     weighted = None
-    for _ in range(ITERS):
+    for step in range(ITERS):
         partial_pred = 0.0
         for s, d, mu in zip(sources, detectors, mu_now):
             scaled = (d * mu[None, :]).astype(BF16)
@@ -69,9 +69,14 @@
         ]
         terms = jnp.stack(ordered(low, *terms)).reshape(2 * cols // 128, 128)
         total = jnp.sum(lax.all_gather(terms, "core", axis=0), axis=0)
-        total = jnp.sum(everywhere(total, REST, 16), axis=0).reshape(2, cols)
-        gradient = [g * grad_scale for g in ordered(low, total[0], total[1])]
-        mu_now = [jnp.maximum(mu - 2.0 * g, 0.0) for mu, g in zip(mu_now, gradient)]
+        if step < ITERS - 1:
+            total = jnp.sum(everywhere(total, REST, 16), axis=0).reshape(2, cols)
+            gradient = ordered(low, total[0], total[1])
+        else:
+            total = jnp.broadcast_to(total.reshape(2, 1, -1, 128), (2, 8, cols // 128, 128))
+            total = lax.all_to_all(total.reshape(16, cols // 128, 128), REST, 0, 0)
+            gradient = [jnp.sum(total, axis=0).reshape(cols)]
+        mu_now = [jnp.maximum(mu - 2.0 * (g * grad_scale), 0.0) for mu, g in zip(mu_now, gradient)]
     return (mu_now[0], weighted)
 
 

time: 149 us -> 148 us (level)
    all_to_all x3 -> x2, blocking collectives: 42.3 us -> 28.2 us  [everywhere(): lax.all_to_all(jnp.broadcast_to(block[None], (count,) + block.shape), axe...]
    all_to_all x0 -> x1, blocking collectives: none -> 13.1 us  [local(): total = lax.all_to_all(total.reshape(16, cols // 128, 128), REST, 0, 0)]
where the time goes in v1:
time: 148 us; the launch traced here: 147 us
  blocking collectives  83.9 us (57%)
  starting transfers between devices  34.9 us (24%)
  waiting for transfers between devices  20.8 us (14%)
  matrix products  3.18 us (2%)
  local copies, waits for them, and re-layouts  1.82 us (1%)
  other arithmetic  1.48 us (1%)
    all_to_all x2, blocking collectives, everywhere(): lax.all_to_all(jnp.broadcast_to(block[None], (count,) + block.shape), axe...  28.2 us
    all_to_all x2, blocking collectives, local(): got = lax.all_to_all(sent, SUM, 0, 0)  27.1 us
    all_to_all x1, blocking collectives, local(): total = lax.all_to_all(total.reshape(16, cols // 128, 128), REST, 0, 0)  13.1 us
    ppermute x1, starting transfers between devices, gather_sources(): lax.ppermute(block, ('z_mid', 'z_hi'), [(0, 1), (1, 3), (2, 0), (3, 2)])  11.8 us
    ppermute x1, waiting for transfers between devices, local(): mu_now = [absorption, lax.ppermute(absorption, 'z_mid', SWAP)]  9.96 us
    ppermute x1, starting transfers between devices, local(): detectors = [detector_fields, lax.ppermute(detector_fields, 'z_mid', SWAP)]  9.96 us
    all_gather x2, blocking collectives, local(): total = jnp.sum(lax.all_gather(terms, 'core', axis=0), axis=0)  9.82 us
    all_to_all x2, starting transfers between devices, everywhere(): lax.all_to_all(jnp.broadcast_to(block[None], (count,) + block.shape), axe...  9.64 us
  transfers between devices with their start and end apart: 6, of which 3 were waited for; matrix products, arithmetic and copies ran while one was open for 0% of the time, Pallas kernels for 0%

profile of v1, /device:TPU:1, one launch (start us, length us, event | category | flops | bytes accessed | tf_op | source)
XLA Modules:
  0.0 147.0 jit_solution(11481922977199973331)
XLA Ops:
  0.6 1.6 %collective-permute-start = (bf16[64,768]{1,0:T(8,128)(2,1)}, bf16[64,768]{1,0:T(8,128)(2,1)S(1)}, u32[]{:S(2)}, u32[]{:S(2)}) collective-permute-start(bf16[64,768]{1,0:T(8,128)(2,1)} %param.6), channel_id=1, source_target_pairs={{0,0},{8,256},{256,8},{264,264},{1,1},{9,257},{257,9},{265,265},{2... | collective-permute-start | bytes 294920 | tf_op jit(solution)/shard_map/ppermute | solution.py:30
  2.2 11.8 %collective-permute-start.1 = (bf16[64,768]{1,0:T(8,128)(2,1)}, bf16[64,768]{1,0:T(8,128)(2,1)S(1)}, u32[]{:S(2)}, u32[]{:S(2)}) collective-permute-start(bf16[64,768]{1,0:T(8,128)(2,1)} %param.6), channel_id=1, source_target_pairs={{0,8},{8,264},{256,0},{264,256},{1,9},{9,265},{257,1},{265,257},{2... | collective-permute-start | bytes 294920 | tf_op jit(solution)/shard_map/ppermute | solution.py:31
  14.0 2.9 %collective-permute-done.1 = bf16[64,768]{1,0:T(8,128)(2,1)S(1)} collective-permute-done((bf16[64,768]{1,0:T(8,128)(2,1)}, bf16[64,768]{1,0:T(8,128)(2,1)S(1)}, u32[]{:S(2)}, u32[]{:S(2)}) %collective-permute-start.1) | collective-permute-done | bytes 98336 | tf_op jit(solution)/shard_map/ppermute | solution.py:31
  17.0 0.9 broadcast_in_dim.12
  17.9 4.1 %all-to-all-start = ((bf16[4,2,64,768]{3,2,1,0:T(8,128)(2,1)}), bf16[4,2,64,768]{3,2,1,0:T(8,128)(2,1)S(1)}, u32[]{:S(2)}, u32[]{:S(2)}) async-start(bf16[4,2,64,768]{3,2,1,0:T(8,128)(2,1)} %broadcast_in_dim.12), calls=%async_computation | async-start | bytes 1572864 | tf_op jit(solution)/shard_map/all_to_all | solution.py:21
  22.1 10.0 %collective-permute-start.2 = (bf16[256,768]{1,0:T(8,128)(2,1)S(1)}, bf16[256,768]{1,0:T(8,128)(2,1)S(1)}, u32[]{:S(2)}, u32[]{:S(2)}) collective-permute-start(bf16[256,768]{1,0:T(8,128)(2,1)S(1)} %copy-done), channel_id=1, source_target_pairs={{0,256},{256,0},{1,257},{257,1},{2,258},{258,2},{3,259},{259,3},{4... | collective-permute-start | bytes 1179656 | tf_op jit(solution)/shard_map/ppermute | solution.py:49
  32.0 1.9 %collective-permute-start.3 = (f32[768]{0:T(1024)S(1)}, f32[768]{0:T(1024)S(1)}, u32[]{:S(2)}, u32[]{:S(2)}) collective-permute-start(f32[768]{0:T(1024)S(1)} %copy-done.4), channel_id=1, source_target_pairs={{0,256},{256,0},{1,257},{257,1},{2,258},{258,2},{3,259},{259,3},{4... | collective-permute-start | bytes 9224 | tf_op jit(solution)/shard_map/ppermute | solution.py:50
  34.0 0.1 fusion.24
  34.0 3.3 %all_gather.12 = bf16[4,2,64,768]{3,2,1,0:T(8,128)(2,1)S(1)} all-gather(bf16[4,1,64,768]{3,2,1,0:T(8,128)(2,1)S(1)} %get-tuple-element.4), channel_id=1, replica_groups=mesh['z_mid'=2,'z_low'=2,'y'=8,'z_hi'=2,'x'=4,'core'=2] {'core'}, dimensions={1}, use_global_device_ids=true | all-gather | bytes 1179648 | tf_op jit(solution)/shard_map/all_gather | solution.py:35
  37.4 0.4 fusion.14
  37.8 2.4 %all_gather.13 = bf16[4,2,64,768]{3,2,1,0:T(8,128)(2,1)S(1)} all-gather(bf16[4,1,64,768]{3,2,1,0:T(8,128)(2,1)S(1)} %get-tuple-element.5), channel_id=1, replica_groups=mesh['z_mid'=2,'z_low'=2,'y'=8,'z_hi'=2,'x'=4,'core'=2] {'core'}, dimensions={1}, use_global_device_ids=true | all-gather | bytes 1179648 | tf_op jit(solution)/shard_map/all_gather | solution.py:35
  40.1 10.0 %collective-permute-done.3 = f32[768]{0:T(1024)S(1)} collective-permute-done((f32[768]{0:T(1024)S(1)}, f32[768]{0:T(1024)S(1)}, u32[]{:S(2)}, u32[]{:S(2)}) %collective-permute-start.3) | collective-permute-done | bytes 3104 | tf_op jit(solution)/shard_map/ppermute | solution.py:50
  50.1 0.4 fusion.4
  50.5 0.0 copy-start.2
  50.6 15.6 %all_to_all.35 = bf16[16,32,256]{2,1,0:T(8,128)(2,1)S(1)} all-to-all(bf16[16,32,256]{2,1,0:T(8,128)(2,1)S(1)} %bitcast.44), channel_id=1, replica_groups=mesh['z_mid'=2,'z_low'=2,'y'=8,'z_hi'=2,'x'=4,'core'=2] {'z_low','y'}, dimensions={0} | all-to-all | bytes 524288 | tf_op jit(solution)/shard_map/all_to_all | solution.py:61
  66.3 0.7 broadcast_in_dim.13
  67.0 5.5 %all-to-all-start.2 = ((bf16[16,32,256]{2,1,0:T(8,128)(2,1)}), bf16[16,32,256]{2,1,0:T(8,128)(2,1)S(1)}, u32[]{:S(2)}, u32[]{:S(2)}) async-start(bf16[16,32,256]{2,1,0:T(8,128)(2,1)} %broadcast_in_dim.13), calls=%async_computation.2 | async-start | bytes 524288 | tf_op jit(solution)/shard_map/all_to_all | solution.py:21
  72.5 7.9 %all-to-all-done.2 = bf16[16,32,256]{2,1,0:T(8,128)(2,1)S(1)} async-done(((bf16[16,32,256]{2,1,0:T(8,128)(2,1)}), bf16[16,32,256]{2,1,0:T(8,128)(2,1)S(1)}, u32[]{:S(2)}, u32[]{:S(2)}) %all-to-all-start.2) | async-done | bytes 262176 | tf_op jit(solution)/shard_map/all_to_all | solution.py:21
  80.4 0.4 fusion
  80.8 0.4 fusion.2
  81.3 4.7 %all_gather.14 = f32[2,12,128]{2,1,0:T(8,128)S(1)} all-gather(f32[1,12,128]{2,1,0:T(8,128)S(1)} %all_gather_reshape.6), channel_id=1, replica_groups=mesh['z_mid'=2,'z_low'=2,'y'=8,'z_hi'=2,'x'=4,'core'=2] {'core'}, dimensions={0}, use_global_device_ids=true | all-gather | bytes 18432 | tf_op jit(solution)/shard_map/all_gather | solution.py:71
  86.0 15.2 %all_to_all.36 = f32[16,12,128]{2,1,0:T(8,128)S(1)} all-to-all(f32[16,12,128]{2,1,0:T(8,128)S(1)} %broadcast_in_dim.14), channel_id=1, replica_groups=mesh['z_mid'=2,'z_low'=2,'y'=8,'z_hi'=2,'x'=4,'core'=2] {'z_mid','z_hi',..., dimensions={0} | all-to-all | bytes 196608 | tf_op jit(solution)/shard_map/all_to_all | solution.py:21
  101.3 0.4 fusion.12
  101.7 0.4 fusion.5
  102.1 11.5 %all_to_all.37 = bf16[16,32,256]{2,1,0:T(8,128)(2,1)S(1)} all-to-all(bf16[16,32,256]{2,1,0:T(8,128)(2,1)S(1)} %bitcast.43), channel_id=1, replica_groups=mesh['z_mid'=2,'z_low'=2,'y'=8,'z_hi'=2,'x'=4,'core'=2] {'z_low','y'}, dimensions={0} | all-to-all | bytes 524288 | tf_op jit(solution)/shard_map/all_to_all | solution.py:61
  113.6 0.6 fusion.23
  114.3 13.0 %all_to_all.38 = bf16[16,32,256]{2,1,0:T(8,128)(2,1)S(1)} all-to-all(bf16[16,32,256]{2,1,0:T(8,128)(2,1)S(1)} %broadcast_in_dim.15), channel_id=1, replica_groups=mesh['z_mid'=2,'z_low'=2,'y'=8,'z_hi'=2,'x'=4,'core'=2] {'z_low','y'}, dimensions={0} | all-to-all | bytes 524288 | tf_op jit(solution)/shard_map/all_to_all | solution.py:21
  127.3 0.4 fusion.1
  127.7 0.4 fusion.3
  128.1 5.1 %all_gather.15 = f32[2,12,128]{2,1,0:T(8,128)S(1)} all-gather(f32[1,12,128]{2,1,0:T(8,128)S(1)} %all_gather_reshape.7), channel_id=1, replica_groups=mesh['z_mid'=2,'z_low'=2,'y'=8,'z_hi'=2,'x'=4,'core'=2] {'core'}, dimensions={0}, use_global_device_ids=true | all-gather | bytes 18432 | tf_op jit(solution)/shard_map/all_gather | solution.py:71
  133.3 13.1 %all_to_all.39 = f32[16,6,128]{2,1,0:T(8,128)S(1)} all-to-all(f32[16,6,128]{2,1,0:T(8,128)S(1)} %bitcast.49), channel_id=1, replica_groups=mesh['z_mid'=2,'z_low'=2,'y'=8,'z_hi'=2,'x'=4,'core'=2] {'z_mid','z_hi',..., dimensions={0} | all-to-all | bytes 98304 | tf_op jit(solution)/shard_map/all_to_all | solution.py:77
  146.4 0.6 fusion.20
  (36 shorter events, 0.4 us)
Async XLA Ops:
  0.6 13.4 %collective-permute-start = (bf16[64,768]{1,0:T(8,128)(2,1)}, bf16[64,768]{1,0:T(8,128)(2,1)S(1)}, u32[]{:S(2)}, u32[]{:S(2)}) collective-permute-start(bf16[64,768]{1,0:T(8,128)(2,1)} %param.6), channel_id=1, source_target_pairs={{0,0},{8,256},{256,8},{264,264},{1,1},{9,257},{257,9},{265,265},{2... | collective-permute-start | bytes 294920 | tf_op jit(solution)/shard_map/ppermute | solution.py:30
  2.2 14.7 %collective-permute-start.1 = (bf16[64,768]{1,0:T(8,128)(2,1)}, bf16[64,768]{1,0:T(8,128)(2,1)S(1)}, u32[]{:S(2)}, u32[]{:S(2)}) collective-permute-start(bf16[64,768]{1,0:T(8,128)(2,1)} %param.6), channel_id=1, source_target_pairs={{0,8},{8,264},{256,0},{264,256},{1,9},{9,265},{257,1},{265,257},{2... | collective-permute-start | bytes 294920 | tf_op jit(solution)/shard_map/ppermute | solution.py:31
  17.9 4.2 %copy-start = (bf16[256,768]{1,0:T(8,128)(2,1)S(1)}, bf16[256,768]{1,0:T(8,128)(2,1)}, u32[]{:S(2)}) copy-start(bf16[256,768]{1,0:T(8,128)(2,1)} %param.7) | copy-start | bytes 1179652
  17.9 14.1 %copy-start.4 = (f32[768]{0:T(1024)S(1)}, f32[768]{0:T(1024)}, u32[]{:S(2)}) copy-start(f32[768]{0:T(1024)} %param.11) | copy-start | bytes 9220
  17.9 16.1 %all-to-all-start = ((bf16[4,2,64,768]{3,2,1,0:T(8,128)(2,1)}), bf16[4,2,64,768]{3,2,1,0:T(8,128)(2,1)S(1)}, u32[]{:S(2)}, u32[]{:S(2)}) async-start(bf16[4,2,64,768]{3,2,1,0:T(8,128)(2,1)} %broadcast_in_dim.12), calls=%async_computation | async-start | bytes 1572864 | tf_op jit(solution)/shard_map/all_to_all | solution.py:21
  22.1 28.0 %collective-permute-start.2 = (bf16[256,768]{1,0:T(8,128)(2,1)S(1)}, bf16[256,768]{1,0:T(8,128)(2,1)S(1)}, u32[]{:S(2)}, u32[]{:S(2)}) collective-permute-start(bf16[256,768]{1,0:T(8,128)(2,1)S(1)} %copy-done), channel_id=1, source_target_pairs={{0,256},{256,0},{1,257},{257,1},{2,258},{258,2},{3,259},{259,3},{4... | collective-permute-start | bytes 1179656 | tf_op jit(solution)/shard_map/ppermute | solution.py:49
  32.0 18.1 %collective-permute-start.3 = (f32[768]{0:T(1024)S(1)}, f32[768]{0:T(1024)S(1)}, u32[]{:S(2)}, u32[]{:S(2)}) collective-permute-start(f32[768]{0:T(1024)S(1)} %copy-done.4), channel_id=1, source_target_pairs={{0,256},{256,0},{1,257},{257,1},{2,258},{258,2},{3,259},{259,3},{4... | collective-permute-start | bytes 9224 | tf_op jit(solution)/shard_map/ppermute | solution.py:50
  50.5 15.7 %copy-start.1 = (f32[32,256]{1,0:T(8,128)S(1)}, f32[32,256]{1,0:T(8,128)}, u32[]{:S(2)}) copy-start(f32[32,256]{1,0:T(8,128)} %param.8) | copy-start | bytes 98308
  50.5 15.7 %copy-start.2 = (s32[32,256]{1,0:T(8,128)S(1)}, s32[32,256]{1,0:T(8,128)}, u32[]{:S(2)}) copy-start(s32[32,256]{1,0:T(8,128)} %param.10) | copy-start | bytes 98308
  50.5 15.7 %copy-start.3 = (s32[32,256]{1,0:T(8,128)S(1)}, s32[32,256]{1,0:T(8,128)}, u32[]{:S(2)}) copy-start(s32[32,256]{1,0:T(8,128)} %param.9) | copy-start | bytes 98308
  67.0 13.4 %all-to-all-start.2 = ((bf16[16,32,256]{2,1,0:T(8,128)(2,1)}), bf16[16,32,256]{2,1,0:T(8,128)(2,1)S(1)}, u32[]{:S(2)}, u32[]{:S(2)}) async-start(bf16[16,32,256]{2,1,0:T(8,128)(2,1)} %broadcast_in_dim.13), calls=%async_computation.2 | async-start | bytes 524288 | tf_op jit(solution)/shard_map/all_to_all | solution.py:21

commit v2 on v1

--- a/solution.py
+++ b/solution.py
@@ -25,15 +25,17 @@
     return jnp.where(first, own, other), jnp.where(first, other, own)
 
 
-def gather_sources(block, aligned):
+def gather_sources(block, aligned, low):
     rows, cols = block.shape
     first = lax.ppermute(block, ("z_mid", "z_hi"), [(0, 0), (1, 2), (2, 1), (3, 3)])
     second = lax.ppermute(block, ("z_mid", "z_hi"), [(0, 1), (1, 3), (2, 0), (3, 2)])
     pieces = jnp.stack(ordered(aligned, first, second))
+    pieces, low = lax.optimization_barrier((pieces, low))
     along = everywhere(pieces, "x", 4)
-    return [
+    gathered = [
         lax.all_gather(along[:, k], "core", axis=1).reshape(8 * rows, cols) for k in range(2)
     ]
+    return gathered, low
 
 
 def local(source_fields, detector_fields, measured, valid_pair, weight_class, absorption):
@@ -42,10 +44,10 @@
     own_rows, own_cols = measured.shape
     pred_scale = 1.0 / jnp.sqrt(jnp.float32(voxels))
     grad_scale = jnp.sqrt(jnp.float32(voxels)) / (jnp.float32(NS) * jnp.float32(ND))
-    low = lax.axis_index("z_mid") == 0
     maskf = valid_pair.astype(jnp.float32) / (1.0 + weight_class.astype(jnp.float32))
 
-    sources = gather_sources(source_fields, lax.axis_index("z_mid") == lax.axis_index("z_hi"))
+    aligned = lax.axis_index("z_mid") == lax.axis_index("z_hi")
+    sources, low = gather_sources(source_fields, aligned, lax.axis_index("z_mid") == 0)
     detectors = [detector_fields, lax.ppermute(detector_fields, "z_mid", SWAP)]
     mu_now = [absorption, lax.ppermute(absorption, "z_mid", SWAP)]
 

time: 148 us -> 147 us (level)
  blocking collectives: 83.9 us -> 97.1 us
  waiting for transfers between devices: 20.8 us -> 12.8 us
  starting transfers between devices: 34.9 us -> 29.4 us
    all_to_all x2 -> x3, blocking collectives: 28.2 us -> 41.4 us  [everywhere(): lax.all_to_all(jnp.broadcast_to(block[None], (count,) + block.shape), axe...]
    all_to_all x2 -> x1, waiting for transfers between devices: 7.9 us -> 0.01 us  [everywhere(): lax.all_to_all(jnp.broadcast_to(block[None], (count,) + block.shape), axe...]
    all_to_all x2 -> x1, starting transfers between devices: 9.64 us -> 4.14 us  [everywhere(): lax.all_to_all(jnp.broadcast_to(block[None], (count,) + block.shape), axe...]
  transfers between devices with their start and end apart: 6 -> 5, of which waited for: 3 -> 2; matrix products, arithmetic and copies ran while one was open for 0% -> 0% of each run, Pallas kernels for 0% -> 0%
where the time goes in v2:
time: 147 us; the launch traced here: 146 us
  blocking collectives  97.1 us (66%)
  starting transfers between devices  29.4 us (20%)
  waiting for transfers between devices  12.8 us (9%)
  matrix products  3.18 us (2%)
  other arithmetic  1.48 us (1%)
    all_to_all x3, blocking collectives, everywhere(): lax.all_to_all(jnp.broadcast_to(block[None], (count,) + block.shape), axe...  41.4 us
    all_to_all x2, blocking collectives, local(): got = lax.all_to_all(sent, SUM, 0, 0)  27.1 us
    all_to_all x1, blocking collectives, local(): total = lax.all_to_all(total.reshape(16, cols // 128, 128), REST, 0, 0)  13.1 us
    ppermute x1, starting transfers between devices, gather_sources(): lax.ppermute(block, ('z_mid', 'z_hi'), [(0, 1), (1, 3), (2, 0), (3, 2)])  11.8 us
    ppermute x1, starting transfers between devices, local(): detectors = [detector_fields, lax.ppermute(detector_fields, 'z_mid', SWAP)]  9.96 us
    ppermute x1, waiting for transfers between devices, local(): mu_now = [absorption, lax.ppermute(absorption, 'z_mid', SWAP)]  9.96 us
    all_gather x2, blocking collectives, local(): total = jnp.sum(lax.all_gather(terms, 'core', axis=0), axis=0)  9.82 us
    all_gather x2, blocking collectives, gather_sources(): lax.all_gather(along[:, k], 'core', axis=1).reshape(8 * rows, cols)  5.69 us
  transfers between devices with their start and end apart: 5, of which 2 were waited for; matrix products, arithmetic and copies ran while one was open for 0% of the time, Pallas kernels for 0%

profile of v2, /device:TPU:1, one launch (start us, length us, event | category | flops | bytes accessed | tf_op | source)
XLA Modules:
  0.0 146.1 jit_solution(6695452113484724025)
XLA Ops:
  0.6 1.6 %collective-permute-start = (bf16[64,768]{1,0:T(8,128)(2,1)}, bf16[64,768]{1,0:T(8,128)(2,1)S(1)}, u32[]{:S(2)}, u32[]{:S(2)}) collective-permute-start(bf16[64,768]{1,0:T(8,128)(2,1)} %param.6), channel_id=1, source_target_pairs={{0,0},{8,256},{256,8},{264,264},{1,1},{9,257},{257,9},{265,265},{2... | collective-permute-start | bytes 294920 | tf_op jit(solution)/shard_map/ppermute | solution.py:30
  2.2 11.8 %collective-permute-start.1 = (bf16[64,768]{1,0:T(8,128)(2,1)}, bf16[64,768]{1,0:T(8,128)(2,1)S(1)}, u32[]{:S(2)}, u32[]{:S(2)}) collective-permute-start(bf16[64,768]{1,0:T(8,128)(2,1)} %param.6), channel_id=1, source_target_pairs={{0,8},{8,264},{256,0},{264,256},{1,9},{9,265},{257,1},{265,257},{2... | collective-permute-start | bytes 294920 | tf_op jit(solution)/shard_map/ppermute | solution.py:31
  14.0 2.9 %collective-permute-done.1 = bf16[64,768]{1,0:T(8,128)(2,1)S(1)} collective-permute-done((bf16[64,768]{1,0:T(8,128)(2,1)}, bf16[64,768]{1,0:T(8,128)(2,1)S(1)}, u32[]{:S(2)}, u32[]{:S(2)}) %collective-permute-start.1) | collective-permute-done | bytes 98336 | tf_op jit(solution)/shard_map/ppermute | solution.py:31
  17.0 0.9 broadcast_in_dim.12
  17.9 4.1 %all-to-all-start = ((bf16[4,2,64,768]{3,2,1,0:T(8,128)(2,1)}), bf16[4,2,64,768]{3,2,1,0:T(8,128)(2,1)S(1)}, u32[]{:S(2)}, u32[]{:S(2)}) async-start(bf16[4,2,64,768]{3,2,1,0:T(8,128)(2,1)} %broadcast_in_dim.12), calls=%async_computation | async-start | bytes 1572864 | tf_op jit(solution)/shard_map/all_to_all | solution.py:21
  22.1 10.0 %collective-permute-start.2 = (bf16[256,768]{1,0:T(8,128)(2,1)S(1)}, bf16[256,768]{1,0:T(8,128)(2,1)S(1)}, u32[]{:S(2)}, u32[]{:S(2)}) collective-permute-start(bf16[256,768]{1,0:T(8,128)(2,1)S(1)} %copy-done), channel_id=1, source_target_pairs={{0,256},{256,0},{1,257},{257,1},{2,258},{258,2},{3,259},{259,3},{4... | collective-permute-start | bytes 1179656 | tf_op jit(solution)/shard_map/ppermute | solution.py:51
  32.0 1.9 %collective-permute-start.3 = (f32[768]{0:T(1024)S(1)}, f32[768]{0:T(1024)S(1)}, u32[]{:S(2)}, u32[]{:S(2)}) collective-permute-start(f32[768]{0:T(1024)S(1)} %copy-done.4), channel_id=1, source_target_pairs={{0,256},{256,0},{1,257},{257,1},{2,258},{258,2},{3,259},{259,3},{4... | collective-permute-start | bytes 9224 | tf_op jit(solution)/shard_map/ppermute | solution.py:52
  34.0 0.1 fusion.24
  34.0 3.3 %all_gather.12 = bf16[4,2,64,768]{3,2,1,0:T(8,128)(2,1)S(1)} all-gather(bf16[4,1,64,768]{3,2,1,0:T(8,128)(2,1)S(1)} %get-tuple-element.8), channel_id=1, replica_groups=mesh['z_mid'=2,'z_low'=2,'y'=8,'z_hi'=2,'x'=4,'core'=2] {'core'}, dimensions={1}, use_global_device_ids=true | all-gather | bytes 1179648 | tf_op jit(solution)/shard_map/all_gather | solution.py:36
  37.4 0.4 fusion.14
  37.8 2.4 %all_gather.13 = bf16[4,2,64,768]{3,2,1,0:T(8,128)(2,1)S(1)} all-gather(bf16[4,1,64,768]{3,2,1,0:T(8,128)(2,1)S(1)} %get-tuple-element.9), channel_id=1, replica_groups=mesh['z_mid'=2,'z_low'=2,'y'=8,'z_hi'=2,'x'=4,'core'=2] {'core'}, dimensions={1}, use_global_device_ids=true | all-gather | bytes 1179648 | tf_op jit(solution)/shard_map/all_gather | solution.py:36
  40.1 10.0 %collective-permute-done.3 = f32[768]{0:T(1024)S(1)} collective-permute-done((f32[768]{0:T(1024)S(1)}, f32[768]{0:T(1024)S(1)}, u32[]{:S(2)}, u32[]{:S(2)}) %collective-permute-start.3) | collective-permute-done | bytes 3104 | tf_op jit(solution)/shard_map/ppermute | solution.py:52
  50.1 0.4 fusion.4
  50.5 0.0 copy-start.1
  50.5 0.0 copy-start.2
  50.5 0.0 copy-start.3
  50.6 15.6 %all_to_all.35 = bf16[16,32,256]{2,1,0:T(8,128)(2,1)S(1)} all-to-all(bf16[16,32,256]{2,1,0:T(8,128)(2,1)S(1)} %bitcast.44), channel_id=1, replica_groups=mesh['z_mid'=2,'z_low'=2,'y'=8,'z_hi'=2,'x'=4,'core'=2] {'z_low','y'}, dimensions={0} | all-to-all | bytes 524288 | tf_op jit(solution)/shard_map/all_to_all | solution.py:63
  66.3 13.2 %all_to_all.36 = bf16[16,32,256]{2,1,0:T(8,128)(2,1)S(1)} all-to-all(bf16[16,32,256]{2,1,0:T(8,128)(2,1)S(1)} %broadcast_in_dim.13), channel_id=1, replica_groups=mesh['z_mid'=2,'z_low'=2,'y'=8,'z_hi'=2,'x'=4,'core'=2] {'z_low','y'}, dimensions={0} | all-to-all | bytes 524288 | tf_op jit(solution)/shard_map/all_to_all | solution.py:21
  79.5 0.4 fusion
  79.9 0.4 fusion.2
  80.4 4.7 %all_gather.14 = f32[2,12,128]{2,1,0:T(8,128)S(1)} all-gather(f32[1,12,128]{2,1,0:T(8,128)S(1)} %all_gather_reshape.6), channel_id=1, replica_groups=mesh['z_mid'=2,'z_low'=2,'y'=8,'z_hi'=2,'x'=4,'core'=2] {'core'}, dimensions={0}, use_global_device_ids=true | all-gather | bytes 18432 | tf_op jit(solution)/shard_map/all_gather | solution.py:73
  85.1 15.2 %all_to_all.37 = f32[16,12,128]{2,1,0:T(8,128)S(1)} all-to-all(f32[16,12,128]{2,1,0:T(8,128)S(1)} %broadcast_in_dim.14), channel_id=1, replica_groups=mesh['z_mid'=2,'z_low'=2,'y'=8,'z_hi'=2,'x'=4,'core'=2] {'z_mid','z_hi',..., dimensions={0} | all-to-all | bytes 196608 | tf_op jit(solution)/shard_map/all_to_all | solution.py:21
  100.4 0.4 fusion.12
  100.8 0.4 fusion.5
  101.2 11.5 %all_to_all.38 = bf16[16,32,256]{2,1,0:T(8,128)(2,1)S(1)} all-to-all(bf16[16,32,256]{2,1,0:T(8,128)(2,1)S(1)} %bitcast.43), channel_id=1, replica_groups=mesh['z_mid'=2,'z_low'=2,'y'=8,'z_hi'=2,'x'=4,'core'=2] {'z_low','y'}, dimensions={0} | all-to-all | bytes 524288 | tf_op jit(solution)/shard_map/all_to_all | solution.py:63
  112.7 0.6 fusion.23
  113.4 13.0 %all_to_all.39 = bf16[16,32,256]{2,1,0:T(8,128)(2,1)S(1)} all-to-all(bf16[16,32,256]{2,1,0:T(8,128)(2,1)S(1)} %broadcast_in_dim.15), channel_id=1, replica_groups=mesh['z_mid'=2,'z_low'=2,'y'=8,'z_hi'=2,'x'=4,'core'=2] {'z_low','y'}, dimensions={0} | all-to-all | bytes 524288 | tf_op jit(solution)/shard_map/all_to_all | solution.py:21
  126.4 0.4 fusion.1
  126.8 0.4 fusion.3
  127.2 5.1 %all_gather.15 = f32[2,12,128]{2,1,0:T(8,128)S(1)} all-gather(f32[1,12,128]{2,1,0:T(8,128)S(1)} %all_gather_reshape.7), channel_id=1, replica_groups=mesh['z_mid'=2,'z_low'=2,'y'=8,'z_hi'=2,'x'=4,'core'=2] {'core'}, dimensions={0}, use_global_device_ids=true | all-gather | bytes 18432 | tf_op jit(solution)/shard_map/all_gather | solution.py:73
  132.4 13.1 %all_to_all.40 = f32[16,6,128]{2,1,0:T(8,128)S(1)} all-to-all(f32[16,6,128]{2,1,0:T(8,128)S(1)} %bitcast.49), channel_id=1, replica_groups=mesh['z_mid'=2,'z_low'=2,'y'=8,'z_hi'=2,'x'=4,'core'=2] {'z_mid','z_hi',..., dimensions={0} | all-to-all | bytes 98304 | tf_op jit(solution)/shard_map/all_to_all | solution.py:79
  145.5 0.6 fusion.20
  (35 shorter events, 0.4 us)
Async XLA Ops:
  0.6 13.4 %collective-permute-start = (bf16[64,768]{1,0:T(8,128)(2,1)}, bf16[64,768]{1,0:T(8,128)(2,1)S(1)}, u32[]{:S(2)}, u32[]{:S(2)}) collective-permute-start(bf16[64,768]{1,0:T(8,128)(2,1)} %param.6), channel_id=1, source_target_pairs={{0,0},{8,256},{256,8},{264,264},{1,1},{9,257},{257,9},{265,265},{2... | collective-permute-start | bytes 294920 | tf_op jit(solution)/shard_map/ppermute | solution.py:30
  2.2 14.7 %collective-permute-start.1 = (bf16[64,768]{1,0:T(8,128)(2,1)}, bf16[64,768]{1,0:T(8,128)(2,1)S(1)}, u32[]{:S(2)}, u32[]{:S(2)}) collective-permute-start(bf16[64,768]{1,0:T(8,128)(2,1)} %param.6), channel_id=1, source_target_pairs={{0,8},{8,264},{256,0},{264,256},{1,9},{9,265},{257,1},{265,257},{2... | collective-permute-start | bytes 294920 | tf_op jit(solution)/shard_map/ppermute | solution.py:31
  17.9 4.2 %copy-start = (bf16[256,768]{1,0:T(8,128)(2,1)S(1)}, bf16[256,768]{1,0:T(8,128)(2,1)}, u32[]{:S(2)}) copy-start(bf16[256,768]{1,0:T(8,128)(2,1)} %param.7) | copy-start | bytes 1179652
  17.9 14.1 %copy-start.4 = (f32[768]{0:T(1024)S(1)}, f32[768]{0:T(1024)}, u32[]{:S(2)}) copy-start(f32[768]{0:T(1024)} %param.11) | copy-start | bytes 9220
  17.9 16.1 %all-to-all-start = ((bf16[4,2,64,768]{3,2,1,0:T(8,128)(2,1)}), bf16[4,2,64,768]{3,2,1,0:T(8,128)(2,1)S(1)}, u32[]{:S(2)}, u32[]{:S(2)}) async-start(bf16[4,2,64,768]{3,2,1,0:T(8,128)(2,1)} %broadcast_in_dim.12), calls=%async_computation | async-start | bytes 1572864 | tf_op jit(solution)/shard_map/all_to_all | solution.py:21
  22.1 28.0 %collective-permute-start.2 = (bf16[256,768]{1,0:T(8,128)(2,1)S(1)}, bf16[256,768]{1,0:T(8,128)(2,1)S(1)}, u32[]{:S(2)}, u32[]{:S(2)}) collective-permute-start(bf16[256,768]{1,0:T(8,128)(2,1)S(1)} %copy-done), channel_id=1, source_target_pairs={{0,256},{256,0},{1,257},{257,1},{2,258},{258,2},{3,259},{259,3},{4... | collective-permute-start | bytes 1179656 | tf_op jit(solution)/shard_map/ppermute | solution.py:51
  32.0 18.1 %collective-permute-start.3 = (f32[768]{0:T(1024)S(1)}, f32[768]{0:T(1024)S(1)}, u32[]{:S(2)}, u32[]{:S(2)}) collective-permute-start(f32[768]{0:T(1024)S(1)} %copy-done.4), channel_id=1, source_target_pairs={{0,256},{256,0},{1,257},{257,1},{2,258},{258,2},{3,259},{259,3},{4... | collective-permute-start | bytes 9224 | tf_op jit(solution)/shard_map/ppermute | solution.py:52
  50.5 15.7 %copy-start.1 = (f32[32,256]{1,0:T(8,128)S(1)}, f32[32,256]{1,0:T(8,128)}, u32[]{:S(2)}) copy-start(f32[32,256]{1,0:T(8,128)} %param.8) | copy-start | bytes 98308
  50.5 15.7 %copy-start.2 = (s32[32,256]{1,0:T(8,128)S(1)}, s32[32,256]{1,0:T(8,128)}, u32[]{:S(2)}) copy-start(s32[32,256]{1,0:T(8,128)} %param.10) | copy-start | bytes 98308
  50.5 15.7 %copy-start.3 = (s32[32,256]{1,0:T(8,128)S(1)}, s32[32,256]{1,0:T(8,128)}, u32[]{:S(2)}) copy-start(s32[32,256]{1,0:T(8,128)} %param.9) | copy-start | bytes 98308

commit v3 on v2

--- a/solution.py
+++ b/solution.py
@@ -69,14 +69,14 @@
             jnp.sum(jnp.dot(all_weighted, d, preferred_element_type=jnp.float32) * s, axis=0)
             for s, d in zip(sources, detectors)
         ]
-        terms = jnp.stack(ordered(low, *terms)).reshape(2 * cols // 128, 128)
+        terms = jnp.stack(ordered(low, *terms)).reshape(1, 2 * cols)
         total = jnp.sum(lax.all_gather(terms, "core", axis=0), axis=0)
         if step < ITERS - 1:
             total = jnp.sum(everywhere(total, REST, 16), axis=0).reshape(2, cols)
             gradient = ordered(low, total[0], total[1])
         else:
-            total = jnp.broadcast_to(total.reshape(2, 1, -1, 128), (2, 8, cols // 128, 128))
-            total = lax.all_to_all(total.reshape(16, cols // 128, 128), REST, 0, 0)
+            total = jnp.broadcast_to(total.reshape(2, 1, cols), (2, 8, cols))
+            total = lax.all_to_all(total.reshape(16, 1, cols), REST, 0, 0)
             gradient = [jnp.sum(total, axis=0).reshape(cols)]
         mu_now = [jnp.maximum(mu - 2.0 * (g * grad_scale), 0.0) for mu, g in zip(mu_now, gradient)]
     return (mu_now[0], weighted)

time: 147 us -> 146 us (level)
  no operation moved by 1% of the time
where the time goes in v3:
time: 146 us; the launch traced here: 145 us
  blocking collectives  95.8 us (66%)
  starting transfers between devices  29.4 us (20%)
  waiting for transfers between devices  12.8 us (9%)
  matrix products  3.18 us (2%)
  other arithmetic  1.61 us (1%)
    all_to_all x3, blocking collectives, everywhere(): lax.all_to_all(jnp.broadcast_to(block[None], (count,) + block.shape), axe...  40.7 us
    all_to_all x2, blocking collectives, local(): got = lax.all_to_all(sent, SUM, 0, 0)  27.3 us
    all_to_all x1, blocking collectives, local(): total = lax.all_to_all(total.reshape(16, 1, cols), REST, 0, 0)  12.3 us
    ppermute x1, starting transfers between devices, gather_sources(): lax.ppermute(block, ('z_mid', 'z_hi'), [(0, 1), (1, 3), (2, 0), (3, 2)])  11.8 us
    ppermute x1, starting transfers between devices, local(): detectors = [detector_fields, lax.ppermute(detector_fields, 'z_mid', SWAP)]  9.96 us
    ppermute x1, waiting for transfers between devices, local(): mu_now = [absorption, lax.ppermute(absorption, 'z_mid', SWAP)]  9.96 us
    all_gather x2, blocking collectives, local(): total = jnp.sum(lax.all_gather(terms, 'core', axis=0), axis=0)  9.81 us
    all_gather x2, blocking collectives, gather_sources(): lax.all_gather(along[:, k], 'core', axis=1).reshape(8 * rows, cols)  5.69 us
  transfers between devices with their start and end apart: 5, of which 2 were waited for; matrix products, arithmetic and copies ran while one was open for 0% of the time, Pallas kernels for 0%

profile of v3, /device:TPU:1, one launch (start us, length us, event | category | flops | bytes accessed | tf_op | source)
XLA Modules:
  0.0 145.1 jit_solution(15158448728589152135)
XLA Ops:
  0.6 1.6 %collective-permute-start = (bf16[64,768]{1,0:T(8,128)(2,1)}, bf16[64,768]{1,0:T(8,128)(2,1)S(1)}, u32[]{:S(2)}, u32[]{:S(2)}) collective-permute-start(bf16[64,768]{1,0:T(8,128)(2,1)} %param.6), channel_id=1, source_target_pairs={{0,0},{8,256},{256,8},{264,264},{1,1},{9,257},{257,9},{265,265},{2... | collective-permute-start | bytes 294920 | tf_op jit(solution)/shard_map/ppermute | solution.py:30
  2.2 11.8 %collective-permute-start.1 = (bf16[64,768]{1,0:T(8,128)(2,1)}, bf16[64,768]{1,0:T(8,128)(2,1)S(1)}, u32[]{:S(2)}, u32[]{:S(2)}) collective-permute-start(bf16[64,768]{1,0:T(8,128)(2,1)} %param.6), channel_id=1, source_target_pairs={{0,8},{8,264},{256,0},{264,256},{1,9},{9,265},{257,1},{265,257},{2... | collective-permute-start | bytes 294920 | tf_op jit(solution)/shard_map/ppermute | solution.py:31
  14.0 2.9 %collective-permute-done.1 = bf16[64,768]{1,0:T(8,128)(2,1)S(1)} collective-permute-done((bf16[64,768]{1,0:T(8,128)(2,1)}, bf16[64,768]{1,0:T(8,128)(2,1)S(1)}, u32[]{:S(2)}, u32[]{:S(2)}) %collective-permute-start.1) | collective-permute-done | bytes 98336 | tf_op jit(solution)/shard_map/ppermute | solution.py:31
  17.0 0.9 broadcast_in_dim.12
  17.9 4.1 %all-to-all-start = ((bf16[4,2,64,768]{3,2,1,0:T(8,128)(2,1)}), bf16[4,2,64,768]{3,2,1,0:T(8,128)(2,1)S(1)}, u32[]{:S(2)}, u32[]{:S(2)}) async-start(bf16[4,2,64,768]{3,2,1,0:T(8,128)(2,1)} %broadcast_in_dim.12), calls=%async_computation | async-start | bytes 1572864 | tf_op jit(solution)/shard_map/all_to_all | solution.py:21
  22.1 10.0 %collective-permute-start.2 = (bf16[256,768]{1,0:T(8,128)(2,1)S(1)}, bf16[256,768]{1,0:T(8,128)(2,1)S(1)}, u32[]{:S(2)}, u32[]{:S(2)}) collective-permute-start(bf16[256,768]{1,0:T(8,128)(2,1)S(1)} %copy-done), channel_id=1, source_target_pairs={{0,256},{256,0},{1,257},{257,1},{2,258},{258,2},{3,259},{259,3},{4... | collective-permute-start | bytes 1179656 | tf_op jit(solution)/shard_map/ppermute | solution.py:51
  32.0 1.9 %collective-permute-start.3 = (f32[768]{0:T(1024)S(1)}, f32[768]{0:T(1024)S(1)}, u32[]{:S(2)}, u32[]{:S(2)}) collective-permute-start(f32[768]{0:T(1024)S(1)} %copy-done.4), channel_id=1, source_target_pairs={{0,256},{256,0},{1,257},{257,1},{2,258},{258,2},{3,259},{259,3},{4... | collective-permute-start | bytes 9224 | tf_op jit(solution)/shard_map/ppermute | solution.py:52
  34.0 0.1 fusion.25
  34.0 3.3 %all_gather.12 = bf16[4,2,64,768]{3,2,1,0:T(8,128)(2,1)S(1)} all-gather(bf16[4,1,64,768]{3,2,1,0:T(8,128)(2,1)S(1)} %get-tuple-element.10), channel_id=1, replica_groups=mesh['z_mid'=2,'z_low'=2,'y'=8,'z_hi'=2,'x'=4,'core'=2] {'core'}, dimensions={1}, use_global_device_ids=true | all-gather | bytes 1179648 | tf_op jit(solution)/shard_map/all_gather | solution.py:36
  37.4 0.4 fusion.14
  37.8 2.4 %all_gather.13 = bf16[4,2,64,768]{3,2,1,0:T(8,128)(2,1)S(1)} all-gather(bf16[4,1,64,768]{3,2,1,0:T(8,128)(2,1)S(1)} %get-tuple-element.11), channel_id=1, replica_groups=mesh['z_mid'=2,'z_low'=2,'y'=8,'z_hi'=2,'x'=4,'core'=2] {'core'}, dimensions={1}, use_global_device_ids=true | all-gather | bytes 1179648 | tf_op jit(solution)/shard_map/all_gather | solution.py:36
  40.1 10.0 %collective-permute-done.3 = f32[768]{0:T(1024)S(1)} collective-permute-done((f32[768]{0:T(1024)S(1)}, f32[768]{0:T(1024)S(1)}, u32[]{:S(2)}, u32[]{:S(2)}) %collective-permute-start.3) | collective-permute-done | bytes 3104 | tf_op jit(solution)/shard_map/ppermute | solution.py:52
  50.1 0.4 fusion.4
  50.6 15.6 %all_to_all.35 = bf16[16,32,256]{2,1,0:T(8,128)(2,1)S(1)} all-to-all(bf16[16,32,256]{2,1,0:T(8,128)(2,1)S(1)} %bitcast.31), channel_id=1, replica_groups=mesh['z_mid'=2,'z_low'=2,'y'=8,'z_hi'=2,'x'=4,'core'=2] {'z_low','y'}, dimensions={0} | all-to-all | bytes 524288 | tf_op jit(solution)/shard_map/all_to_all | solution.py:63
  66.3 13.2 %all_to_all.36 = bf16[16,32,256]{2,1,0:T(8,128)(2,1)S(1)} all-to-all(bf16[16,32,256]{2,1,0:T(8,128)(2,1)S(1)} %broadcast_in_dim.13), channel_id=1, replica_groups=mesh['z_mid'=2,'z_low'=2,'y'=8,'z_hi'=2,'x'=4,'core'=2] {'z_low','y'}, dimensions={0} | all-to-all | bytes 524288 | tf_op jit(solution)/shard_map/all_to_all | solution.py:21
  79.5 0.4 fusion
  79.9 0.4 fusion.2
  80.4 4.7 %all_gather.14 = f32[2,1,1536]{2,1,0:T(1,128)S(1)} all-gather(f32[1,1,1536]{2,1,0:T(1,128)S(1)} %all_gather_reshape.6), channel_id=1, replica_groups=mesh['z_mid'=2,'z_low'=2,'y'=8,'z_hi'=2,'x'=4,'core'=2] {'core'}, dimensions={0}, use_global_device_ids=true | all-gather | bytes 18432 | tf_op jit(solution)/shard_map/all_gather | solution.py:73
  85.1 0.1 broadcast_in_dim.14
  85.2 14.5 %all_to_all.37 = f32[16,1,1536]{2,1,0:T(1,128)S(1)} all-to-all(f32[16,1,1536]{2,1,0:T(1,128)S(1)} %broadcast_in_dim.14), channel_id=1, replica_groups=mesh['z_mid'=2,'z_low'=2,'y'=8,'z_hi'=2,'x'=4,'core'=2] {'z_mid','z_hi',..., dimensions={0} | all-to-all | bytes 196608 | tf_op jit(solution)/shard_map/all_to_all | solution.py:21
  99.7 0.1 reduce_sum.96
  99.8 0.4 fusion.12
  100.2 0.4 fusion.5
  100.7 11.7 %all_to_all.38 = bf16[16,32,256]{2,1,0:T(8,128)(2,1)S(1)} all-to-all(bf16[16,32,256]{2,1,0:T(8,128)(2,1)S(1)} %bitcast.30), channel_id=1, replica_groups=mesh['z_mid'=2,'z_low'=2,'y'=8,'z_hi'=2,'x'=4,'core'=2] {'z_low','y'}, dimensions={0} | all-to-all | bytes 524288 | tf_op jit(solution)/shard_map/all_to_all | solution.py:63
  112.4 0.6 fusion.24
  113.1 13.0 %all_to_all.39 = bf16[16,32,256]{2,1,0:T(8,128)(2,1)S(1)} all-to-all(bf16[16,32,256]{2,1,0:T(8,128)(2,1)S(1)} %broadcast_in_dim.15), channel_id=1, replica_groups=mesh['z_mid'=2,'z_low'=2,'y'=8,'z_hi'=2,'x'=4,'core'=2] {'z_low','y'}, dimensions={0} | all-to-all | bytes 524288 | tf_op jit(solution)/shard_map/all_to_all | solution.py:21
  126.1 0.4 fusion.1
  126.5 0.4 fusion.3
  126.9 5.1 %all_gather.15 = f32[2,1,1536]{2,1,0:T(1,128)S(1)} all-gather(f32[1,1,1536]{2,1,0:T(1,128)S(1)} %all_gather_reshape.7), channel_id=1, replica_groups=mesh['z_mid'=2,'z_low'=2,'y'=8,'z_hi'=2,'x'=4,'core'=2] {'core'}, dimensions={0}, use_global_device_ids=true | all-gather | bytes 18432 | tf_op jit(solution)/shard_map/all_gather | solution.py:73
  132.1 0.1 reshape.116
  132.1 12.3 %all_to_all.40 = f32[16,1,768]{2,1,0:T(1,128)S(1)} all-to-all(f32[16,1,768]{2,1,0:T(1,128)S(1)} %reshape.116), channel_id=1, replica_groups=mesh['z_mid'=2,'z_low'=2,'y'=8,'z_hi'=2,'x'=4,'core'=2] {'z_mid','z_hi',..., dimensions={0} | all-to-all | bytes 98304 | tf_op jit(solution)/shard_map/all_to_all | solution.py:79
  144.5 0.6 subtract_maximum_fusion
  (38 shorter events, 0.5 us)
Async XLA Ops:
  0.6 13.4 %collective-permute-start = (bf16[64,768]{1,0:T(8,128)(2,1)}, bf16[64,768]{1,0:T(8,128)(2,1)S(1)}, u32[]{:S(2)}, u32[]{:S(2)}) collective-permute-start(bf16[64,768]{1,0:T(8,128)(2,1)} %param.6), channel_id=1, source_target_pairs={{0,0},{8,256},{256,8},{264,264},{1,1},{9,257},{257,9},{265,265},{2... | collective-permute-start | bytes 294920 | tf_op jit(solution)/shard_map/ppermute | solution.py:30
  2.2 14.7 %collective-permute-start.1 = (bf16[64,768]{1,0:T(8,128)(2,1)}, bf16[64,768]{1,0:T(8,128)(2,1)S(1)}, u32[]{:S(2)}, u32[]{:S(2)}) collective-permute-start(bf16[64,768]{1,0:T(8,128)(2,1)} %param.6), channel_id=1, source_target_pairs={{0,8},{8,264},{256,0},{264,256},{1,9},{9,265},{257,1},{265,257},{2... | collective-permute-start | bytes 294920 | tf_op jit(solution)/shard_map/ppermute | solution.py:31
  17.9 4.2 %copy-start = (bf16[256,768]{1,0:T(8,128)(2,1)S(1)}, bf16[256,768]{1,0:T(8,128)(2,1)}, u32[]{:S(2)}) copy-start(bf16[256,768]{1,0:T(8,128)(2,1)} %param.7) | copy-start | bytes 1179652
  17.9 14.1 %copy-start.4 = (f32[768]{0:T(1024)S(1)}, f32[768]{0:T(1024)}, u32[]{:S(2)}) copy-start(f32[768]{0:T(1024)} %param.11) | copy-start | bytes 9220
  17.9 16.1 %all-to-all-start = ((bf16[4,2,64,768]{3,2,1,0:T(8,128)(2,1)}), bf16[4,2,64,768]{3,2,1,0:T(8,128)(2,1)S(1)}, u32[]{:S(2)}, u32[]{:S(2)}) async-start(bf16[4,2,64,768]{3,2,1,0:T(8,128)(2,1)} %broadcast_in_dim.12), calls=%async_computation | async-start | bytes 1572864 | tf_op jit(solution)/shard_map/all_to_all | solution.py:21
  22.1 28.0 %collective-permute-start.2 = (bf16[256,768]{1,0:T(8,128)(2,1)S(1)}, bf16[256,768]{1,0:T(8,128)(2,1)S(1)}, u32[]{:S(2)}, u32[]{:S(2)}) collective-permute-start(bf16[256,768]{1,0:T(8,128)(2,1)S(1)} %copy-done), channel_id=1, source_target_pairs={{0,256},{256,0},{1,257},{257,1},{2,258},{258,2},{3,259},{259,3},{4... | collective-permute-start | bytes 1179656 | tf_op jit(solution)/shard_map/ppermute | solution.py:51
  32.0 18.1 %collective-permute-start.3 = (f32[768]{0:T(1024)S(1)}, f32[768]{0:T(1024)S(1)}, u32[]{:S(2)}, u32[]{:S(2)}) collective-permute-start(f32[768]{0:T(1024)S(1)} %copy-done.4), channel_id=1, source_target_pairs={{0,256},{256,0},{1,257},{257,1},{2,258},{258,2},{3,259},{259,3},{4... | collective-permute-start | bytes 9224 | tf_op jit(solution)/shard_map/ppermute | solution.py:52
  50.5 15.7 %copy-start.1 = (f32[32,256]{1,0:T(8,128)S(1)}, f32[32,256]{1,0:T(8,128)}, u32[]{:S(2)}) copy-start(f32[32,256]{1,0:T(8,128)} %param.8) | copy-start | bytes 98308
  50.5 15.7 %copy-start.2 = (s32[32,256]{1,0:T(8,128)S(1)}, s32[32,256]{1,0:T(8,128)}, u32[]{:S(2)}) copy-start(s32[32,256]{1,0:T(8,128)} %param.10) | copy-start | bytes 98308
  50.5 15.7 %copy-start.3 = (s32[32,256]{1,0:T(8,128)S(1)}, s32[32,256]{1,0:T(8,128)}, u32[]{:S(2)}) copy-start(s32[32,256]{1,0:T(8,128)} %param.9) | copy-start | bytes 98308

commit v4 on v3

--- a/solution.py
+++ b/solution.py
@@ -69,11 +69,11 @@
             jnp.sum(jnp.dot(all_weighted, d, preferred_element_type=jnp.float32) * s, axis=0)
             for s, d in zip(sources, detectors)
         ]
-        terms = jnp.stack(ordered(low, *terms)).reshape(1, 2 * cols)
+        terms = jnp.concatenate(ordered(low, *terms))[None]
         total = jnp.sum(lax.all_gather(terms, "core", axis=0), axis=0)
         if step < ITERS - 1:
-            total = jnp.sum(everywhere(total, REST, 16), axis=0).reshape(2, cols)
-            gradient = ordered(low, total[0], total[1])
+            total = jnp.sum(everywhere(total, REST, 16), axis=0)[0]
+            gradient = ordered(low, total[:cols], total[cols:])
         else:
             total = jnp.broadcast_to(total.reshape(2, 1, cols), (2, 8, cols))
             total = lax.all_to_all(total.reshape(16, 1, cols), REST, 0, 0)

time: 146 us -> 146 us (level)
  no operation moved by 1% of the time
where the time goes in v4:
time: 146 us; the launch traced here: 145 us
  blocking collectives  95.8 us (66%)
  starting transfers between devices  29.4 us (20%)
  waiting for transfers between devices  12.8 us (9%)
  matrix products  3.18 us (2%)
  other arithmetic  1.6 us (1%)
    all_to_all x3, blocking collectives, everywhere(): lax.all_to_all(jnp.broadcast_to(block[None], (count,) + block.shape), axe...  40.7 us
    all_to_all x2, blocking collectives, local(): got = lax.all_to_all(sent, SUM, 0, 0)  27.3 us
    all_to_all x1, blocking collectives, local(): total = lax.all_to_all(total.reshape(16, 1, cols), REST, 0, 0)  12.3 us
    ppermute x1, starting transfers between devices, gather_sources(): lax.ppermute(block, ('z_mid', 'z_hi'), [(0, 1), (1, 3), (2, 0), (3, 2)])  11.8 us
    ppermute x1, starting transfers between devices, local(): detectors = [detector_fields, lax.ppermute(detector_fields, 'z_mid', SWAP)]  9.96 us
    ppermute x1, waiting for transfers between devices, local(): mu_now = [absorption, lax.ppermute(absorption, 'z_mid', SWAP)]  9.96 us
    all_gather x2, blocking collectives, local(): total = jnp.sum(lax.all_gather(terms, 'core', axis=0), axis=0)  9.81 us
    all_gather x2, blocking collectives, gather_sources(): lax.all_gather(along[:, k], 'core', axis=1).reshape(8 * rows, cols)  5.69 us
  transfers between devices with their start and end apart: 5, of which 2 were waited for; matrix products, arithmetic and copies ran while one was open for 0% of the time, Pallas kernels for 0%

profile of v4, /device:TPU:1, one launch (start us, length us, event | category | flops | bytes accessed | tf_op | source)
XLA Modules:
  0.0 145.0 jit_solution(1104745077258124521)
XLA Ops:
  0.6 1.6 %collective-permute-start = (bf16[64,768]{1,0:T(8,128)(2,1)}, bf16[64,768]{1,0:T(8,128)(2,1)S(1)}, u32[]{:S(2)}, u32[]{:S(2)}) collective-permute-start(bf16[64,768]{1,0:T(8,128)(2,1)} %param.6), channel_id=1, source_target_pairs={{0,0},{8,256},{256,8},{264,264},{1,1},{9,257},{257,9},{265,265},{2... | collective-permute-start | bytes 294920 | tf_op jit(solution)/shard_map/ppermute | solution.py:30
  2.2 11.8 %collective-permute-start.1 = (bf16[64,768]{1,0:T(8,128)(2,1)}, bf16[64,768]{1,0:T(8,128)(2,1)S(1)}, u32[]{:S(2)}, u32[]{:S(2)}) collective-permute-start(bf16[64,768]{1,0:T(8,128)(2,1)} %param.6), channel_id=1, source_target_pairs={{0,8},{8,264},{256,0},{264,256},{1,9},{9,265},{257,1},{265,257},{2... | collective-permute-start | bytes 294920 | tf_op jit(solution)/shard_map/ppermute | solution.py:31
  14.0 2.9 %collective-permute-done.1 = bf16[64,768]{1,0:T(8,128)(2,1)S(1)} collective-permute-done((bf16[64,768]{1,0:T(8,128)(2,1)}, bf16[64,768]{1,0:T(8,128)(2,1)S(1)}, u32[]{:S(2)}, u32[]{:S(2)}) %collective-permute-start.1) | collective-permute-done | bytes 98336 | tf_op jit(solution)/shard_map/ppermute | solution.py:31
  17.0 0.9 broadcast_in_dim.12
  17.9 4.1 %all-to-all-start = ((bf16[4,2,64,768]{3,2,1,0:T(8,128)(2,1)}), bf16[4,2,64,768]{3,2,1,0:T(8,128)(2,1)S(1)}, u32[]{:S(2)}, u32[]{:S(2)}) async-start(bf16[4,2,64,768]{3,2,1,0:T(8,128)(2,1)} %broadcast_in_dim.12), calls=%async_computation | async-start | bytes 1572864 | tf_op jit(solution)/shard_map/all_to_all | solution.py:21
  22.1 10.0 %collective-permute-start.2 = (bf16[256,768]{1,0:T(8,128)(2,1)S(1)}, bf16[256,768]{1,0:T(8,128)(2,1)S(1)}, u32[]{:S(2)}, u32[]{:S(2)}) collective-permute-start(bf16[256,768]{1,0:T(8,128)(2,1)S(1)} %copy-done), channel_id=1, source_target_pairs={{0,256},{256,0},{1,257},{257,1},{2,258},{258,2},{3,259},{259,3},{4... | collective-permute-start | bytes 1179656 | tf_op jit(solution)/shard_map/ppermute | solution.py:51
  32.0 1.9 %collective-permute-start.3 = (f32[768]{0:T(1024)S(1)}, f32[768]{0:T(1024)S(1)}, u32[]{:S(2)}, u32[]{:S(2)}) collective-permute-start(f32[768]{0:T(1024)S(1)} %copy-done.4), channel_id=1, source_target_pairs={{0,256},{256,0},{1,257},{257,1},{2,258},{258,2},{3,259},{259,3},{4... | collective-permute-start | bytes 9224 | tf_op jit(solution)/shard_map/ppermute | solution.py:52
  34.0 0.1 fusion.25
  34.0 3.3 %all_gather.12 = bf16[4,2,64,768]{3,2,1,0:T(8,128)(2,1)S(1)} all-gather(bf16[4,1,64,768]{3,2,1,0:T(8,128)(2,1)S(1)} %get-tuple-element.10), channel_id=1, replica_groups=mesh['z_mid'=2,'z_low'=2,'y'=8,'z_hi'=2,'x'=4,'core'=2] {'core'}, dimensions={1}, use_global_device_ids=true | all-gather | bytes 1179648 | tf_op jit(solution)/shard_map/all_gather | solution.py:36
  37.4 0.4 fusion.14
  37.8 2.4 %all_gather.13 = bf16[4,2,64,768]{3,2,1,0:T(8,128)(2,1)S(1)} all-gather(bf16[4,1,64,768]{3,2,1,0:T(8,128)(2,1)S(1)} %get-tuple-element.11), channel_id=1, replica_groups=mesh['z_mid'=2,'z_low'=2,'y'=8,'z_hi'=2,'x'=4,'core'=2] {'core'}, dimensions={1}, use_global_device_ids=true | all-gather | bytes 1179648 | tf_op jit(solution)/shard_map/all_gather | solution.py:36
  40.1 10.0 %collective-permute-done.3 = f32[768]{0:T(1024)S(1)} collective-permute-done((f32[768]{0:T(1024)S(1)}, f32[768]{0:T(1024)S(1)}, u32[]{:S(2)}, u32[]{:S(2)}) %collective-permute-start.3) | collective-permute-done | bytes 3104 | tf_op jit(solution)/shard_map/ppermute | solution.py:52
  50.1 0.4 fusion.4
  50.6 15.6 %all_to_all.35 = bf16[16,32,256]{2,1,0:T(8,128)(2,1)S(1)} all-to-all(bf16[16,32,256]{2,1,0:T(8,128)(2,1)S(1)} %bitcast.31), channel_id=1, replica_groups=mesh['z_mid'=2,'z_low'=2,'y'=8,'z_hi'=2,'x'=4,'core'=2] {'z_low','y'}, dimensions={0} | all-to-all | bytes 524288 | tf_op jit(solution)/shard_map/all_to_all | solution.py:63
  66.3 13.2 %all_to_all.36 = bf16[16,32,256]{2,1,0:T(8,128)(2,1)S(1)} all-to-all(bf16[16,32,256]{2,1,0:T(8,128)(2,1)S(1)} %broadcast_in_dim.13), channel_id=1, replica_groups=mesh['z_mid'=2,'z_low'=2,'y'=8,'z_hi'=2,'x'=4,'core'=2] {'z_low','y'}, dimensions={0} | all-to-all | bytes 524288 | tf_op jit(solution)/shard_map/all_to_all | solution.py:21
  79.5 0.4 fusion
  79.9 0.4 fusion.2
  80.4 4.7 %all-gather.2 = f32[2,1,1536]{2,1,0:T(1,128)S(1)} all-gather(f32[1,1,1536]{2,1,0:T(1,128)S(1)} %reshape.66), channel_id=2, replica_groups=mesh['z_mid'=2,'z_low'=2,'y'=8,'z_hi'=2,'x'=4,'core'=2] {'core'}, dimensions={0}, use_global_device_ids=true | all-gather | bytes 18432 | tf_op jit(solution)/shard_map/all_gather | solution.py:73
  85.1 0.1 broadcast_in_dim.14
  85.1 14.5 %all_to_all.37 = f32[16,1,1536]{2,1,0:T(1,128)S(1)} all-to-all(f32[16,1,1536]{2,1,0:T(1,128)S(1)} %broadcast_in_dim.14), channel_id=1, replica_groups=mesh['z_mid'=2,'z_low'=2,'y'=8,'z_hi'=2,'x'=4,'core'=2] {'z_mid','z_hi',..., dimensions={0} | all-to-all | bytes 196608 | tf_op jit(solution)/shard_map/all_to_all | solution.py:21
  99.7 0.1 reduce_sum.96
  99.8 0.4 fusion.12
  100.2 0.4 fusion.5
  100.6 11.7 %all_to_all.38 = bf16[16,32,256]{2,1,0:T(8,128)(2,1)S(1)} all-to-all(bf16[16,32,256]{2,1,0:T(8,128)(2,1)S(1)} %bitcast.30), channel_id=1, replica_groups=mesh['z_mid'=2,'z_low'=2,'y'=8,'z_hi'=2,'x'=4,'core'=2] {'z_low','y'}, dimensions={0} | all-to-all | bytes 524288 | tf_op jit(solution)/shard_map/all_to_all | solution.py:63
  112.4 0.6 fusion.24
  113.0 13.0 %all_to_all.39 = bf16[16,32,256]{2,1,0:T(8,128)(2,1)S(1)} all-to-all(bf16[16,32,256]{2,1,0:T(8,128)(2,1)S(1)} %broadcast_in_dim.15), channel_id=1, replica_groups=mesh['z_mid'=2,'z_low'=2,'y'=8,'z_hi'=2,'x'=4,'core'=2] {'z_low','y'}, dimensions={0} | all-to-all | bytes 524288 | tf_op jit(solution)/shard_map/all_to_all | solution.py:21
  126.0 0.4 fusion.1
  126.4 0.4 fusion.3
  126.9 5.1 %all-gather.3 = f32[2,1,1536]{2,1,0:T(1,128)S(1)} all-gather(f32[1,1,1536]{2,1,0:T(1,128)S(1)} %reshape.68), channel_id=3, replica_groups=mesh['z_mid'=2,'z_low'=2,'y'=8,'z_hi'=2,'x'=4,'core'=2] {'core'}, dimensions={0}, use_global_device_ids=true | all-gather | bytes 18432 | tf_op jit(solution)/shard_map/all_gather | solution.py:73
  132.0 0.1 reshape.61
  132.1 12.3 %all_to_all.40 = f32[16,1,768]{2,1,0:T(1,128)S(1)} all-to-all(f32[16,1,768]{2,1,0:T(1,128)S(1)} %reshape.61), channel_id=1, replica_groups=mesh['z_mid'=2,'z_low'=2,'y'=8,'z_hi'=2,'x'=4,'core'=2] {'z_mid','z_hi',..., dimensions={0} | all-to-all | bytes 98304 | tf_op jit(solution)/shard_map/all_to_all | solution.py:79
  144.4 0.6 subtract_maximum_fusion
  (34 shorter events, 0.4 us)
Async XLA Ops:
  0.6 13.4 %collective-permute-start = (bf16[64,768]{1,0:T(8,128)(2,1)}, bf16[64,768]{1,0:T(8,128)(2,1)S(1)}, u32[]{:S(2)}, u32[]{:S(2)}) collective-permute-start(bf16[64,768]{1,0:T(8,128)(2,1)} %param.6), channel_id=1, source_target_pairs={{0,0},{8,256},{256,8},{264,264},{1,1},{9,257},{257,9},{265,265},{2... | collective-permute-start | bytes 294920 | tf_op jit(solution)/shard_map/ppermute | solution.py:30
  2.2 14.7 %collective-permute-start.1 = (bf16[64,768]{1,0:T(8,128)(2,1)}, bf16[64,768]{1,0:T(8,128)(2,1)S(1)}, u32[]{:S(2)}, u32[]{:S(2)}) collective-permute-start(bf16[64,768]{1,0:T(8,128)(2,1)} %param.6), channel_id=1, source_target_pairs={{0,8},{8,264},{256,0},{264,256},{1,9},{9,265},{257,1},{265,257},{2... | collective-permute-start | bytes 294920 | tf_op jit(solution)/shard_map/ppermute | solution.py:31
  17.9 4.2 %copy-start = (bf16[256,768]{1,0:T(8,128)(2,1)S(1)}, bf16[256,768]{1,0:T(8,128)(2,1)}, u32[]{:S(2)}) copy-start(bf16[256,768]{1,0:T(8,128)(2,1)} %param.7) | copy-start | bytes 1179652
  17.9 14.1 %copy-start.4 = (f32[768]{0:T(1024)S(1)}, f32[768]{0:T(1024)}, u32[]{:S(2)}) copy-start(f32[768]{0:T(1024)} %param.11) | copy-start | bytes 9220
  17.9 16.1 %all-to-all-start = ((bf16[4,2,64,768]{3,2,1,0:T(8,128)(2,1)}), bf16[4,2,64,768]{3,2,1,0:T(8,128)(2,1)S(1)}, u32[]{:S(2)}, u32[]{:S(2)}) async-start(bf16[4,2,64,768]{3,2,1,0:T(8,128)(2,1)} %broadcast_in_dim.12), calls=%async_computation | async-start | bytes 1572864 | tf_op jit(solution)/shard_map/all_to_all | solution.py:21
  22.1 28.0 %collective-permute-start.2 = (bf16[256,768]{1,0:T(8,128)(2,1)S(1)}, bf16[256,768]{1,0:T(8,128)(2,1)S(1)}, u32[]{:S(2)}, u32[]{:S(2)}) collective-permute-start(bf16[256,768]{1,0:T(8,128)(2,1)S(1)} %copy-done), channel_id=1, source_target_pairs={{0,256},{256,0},{1,257},{257,1},{2,258},{258,2},{3,259},{259,3},{4... | collective-permute-start | bytes 1179656 | tf_op jit(solution)/shard_map/ppermute | solution.py:51
  32.0 18.1 %collective-permute-start.3 = (f32[768]{0:T(1024)S(1)}, f32[768]{0:T(1024)S(1)}, u32[]{:S(2)}, u32[]{:S(2)}) collective-permute-start(f32[768]{0:T(1024)S(1)} %copy-done.4), channel_id=1, source_target_pairs={{0,256},{256,0},{1,257},{257,1},{2,258},{258,2},{3,259},{259,3},{4... | collective-permute-start | bytes 9224 | tf_op jit(solution)/shard_map/ppermute | solution.py:52
  50.5 15.7 %copy-start.1 = (f32[32,256]{1,0:T(8,128)S(1)}, f32[32,256]{1,0:T(8,128)}, u32[]{:S(2)}) copy-start(f32[32,256]{1,0:T(8,128)} %param.8) | copy-start | bytes 98308
  50.5 15.7 %copy-start.2 = (s32[32,256]{1,0:T(8,128)S(1)}, s32[32,256]{1,0:T(8,128)}, u32[]{:S(2)}) copy-start(s32[32,256]{1,0:T(8,128)} %param.10) | copy-start | bytes 98308
  50.5 15.7 %copy-start.3 = (s32[32,256]{1,0:T(8,128)S(1)}, s32[32,256]{1,0:T(8,128)}, u32[]{:S(2)}) copy-start(s32[32,256]{1,0:T(8,128)} %param.9) | copy-start | bytes 98308
